TPU v7x, 256 devices: a whole 4x4x8 slice. The times are simulated.
256 devices in a mesh: prompt: 4 (over x), vocab: 64 (over z, y, core).
Axes of the slice: x: 4, y: 4, z: 8, core: 2. Of those that a mesh axis runs over, the one named last changes fastest.
Arguments:
- hidden: bfloat16 [512, 8192], P('prompt')
- head: bfloat16 [8192, 65536], P('prompt', 'vocab')
- gain: float32 [8192], replicated, may hold values from 0.25 to 1.75
- refusal_ids: int32 [512, 16], P('prompt'), may hold values from 0 to 65535, as said below
- refusal_count: int32 [512], P('prompt'), may hold values from 1 to 16
- loss_scale: float32 [512], P('prompt'), may hold values from 8 to 32
Outputs:
- grad_hidden: float32 [512, 8192], P('prompt', 'vocab')
- log_refusal: float32 [512], P('prompt')
Inputs may be any that keep to these rules, and one draw needn't show every extreme that they name: `refusal_ids`: the first refusal_count entries of a prompt's list are distinct ids below 65536; later entries are ignored.
All inputs are finite; a program needn't handle non-finite values.
Results may differ from a plain program's by a relative error of at most 0.0027.
The roundings to bfloat16 on the way count: a program that leaves them out, or rounds other values in their place, can miss the bound.
Values may be sent and summed in bfloat16 or wider, within the bound.
A program may use at most 128 MiB of HBM per device.

v0:
```python
import jax
import jax.numpy as jnp
from jax import lax
from jax.sharding import PartitionSpec as P

epsilon = 1e-05
lowest = -1e30


def shards(hidden, head, gain, refusal_ids, refusal_count, loss_scale):
    row_count, model_width = hidden.shape
    vocab_local = head.shape[1]
    list_length = refusal_ids.shape[1]
    hidden_f = hidden.astype(jnp.float32)
    inverse_rms = lax.rsqrt(jnp.mean(hidden_f * hidden_f, axis=1, keepdims=True) + epsilon)
    normed = (hidden_f * inverse_rms * gain).astype(jnp.bfloat16)
    logits = jnp.dot(
        normed,
        lax.all_gather(head, "prompt", axis=0, tiled=True),
        preferred_element_type=jnp.float32,
    )
    vocab_start = lax.axis_index("vocab") * vocab_local
    shifted_ids = refusal_ids - vocab_start
    in_list = jnp.arange(list_length)[None, :] < refusal_count[:, None]
    is_local = in_list & (shifted_ids >= 0) & (shifted_ids < vocab_local)
    safe_ids = jnp.clip(shifted_ids, 0, vocab_local - 1)
    picked = jnp.take_along_axis(logits, safe_ids, axis=1)
    peak_all = jnp.max(logits, axis=1)
    peak_ref = jnp.max(jnp.where(is_local, picked, lowest), axis=1)
    peak_all, peak_ref = lax.pmax((peak_all, peak_ref), "vocab")
    sum_all = jnp.sum(jnp.exp(logits - peak_all[:, None]), axis=1)
    sum_ref = jnp.sum(jnp.exp(jnp.where(is_local, picked - peak_ref[:, None], lowest)), axis=1)
    sum_all, sum_ref = lax.psum((sum_all, sum_ref), "vocab")
    lse_all = peak_all + jnp.log(sum_all)
    lse_ref = peak_ref + jnp.log(sum_ref)
    log_refusal = lse_ref - lse_all
    member = jnp.any(
        (safe_ids[:, :, None] == jnp.arange(vocab_local)[None, None, :]) & is_local[:, :, None],
        axis=1,
    )
    grad_logits = loss_scale[:, None] * (
        jnp.exp(jnp.where(member, logits - lse_ref[:, None], lowest))
        - jnp.exp(logits - lse_all[:, None])
    )
    grad_b = grad_logits.astype(jnp.bfloat16)
    slice_width = model_width // lax.axis_size("vocab")
    col_start = lax.axis_index("vocab") * slice_width
    grad_full = lax.dot_general(
        grad_b,
        lax.all_gather(head, "prompt", axis=0, tiled=True),
        (((1,), (1,)), ((), ())),
        preferred_element_type=jnp.float32,
    )
    grad_cols = lax.psum_scatter(grad_full, "vocab", scatter_dimension=1, tiled=True)
    normed_cols = lax.dynamic_slice_in_dim(normed, col_start, slice_width, 1).astype(jnp.float32)
    row_term = lax.psum(jnp.sum(grad_cols * normed_cols, axis=1), "vocab")
    hidden_cols = lax.dynamic_slice_in_dim(hidden_f, col_start, slice_width, 1)
    gain_cols = lax.dynamic_slice_in_dim(gain, col_start, slice_width, 0)
    grad_hidden = (
        inverse_rms * gain_cols * grad_cols
        - hidden_cols * (inverse_rms * inverse_rms / model_width) * row_term[:, None]
    )
    return (grad_hidden, log_refusal)


def solution(mesh):
    return jax.shard_map(
        shards,
        mesh=mesh,
        in_specs=(
            P("prompt", None),
            P("prompt", "vocab"),
            P(),
            P("prompt", None),
            P("prompt"),
            P("prompt"),
        ),
        out_specs=(P("prompt", "vocab"), P("prompt")),
        check_vma=False,
    )
```

profile of v0, /device:TPU:1, one launch (start us, length us, event | category | flops | bytes accessed | tf_op | source)
XLA Modules:
  0.0 739.2 jit_solution(6245504685200072266)
XLA Ops:
  7.2 0.0 copy-start.2
  7.2 0.0 copy-start
  7.2 0.0 copy-start.1
  7.2 0.0 all-gather.2.cloned.1.call-start
  7.2 0.7 all-gather.2.cloned.1.call-update
  7.9 0.0 reduce-scatter.2.cloned.1.call-start
  8.0 0.0 copy-done.2
  8.0 0.1 copy.11
  8.1 0.1 reshape.39
  8.2 0.6 copy-done
  8.8 0.5 multiply_reduce_fusion
  9.3 0.0 copy-done.1
  9.3 1.9 multiply_convert_fusion
  11.2 159.1 %all-gather.2.cloned.1.call-done = bf16[8192,1024]{1,0:T(8,128)(2,1)} async-done(((bf16[2048,1024]{1,0:T(8,128)(2,1)}), bf16[8192,1024]{1,0:T(8,128)(2,1)}) %all-gather.2.cloned.1.call-update) | async-done | bytes 16777232 | tf_op jit(solution)/shard_map/all_gather | solution.py:19
  170.3 8.8 %fusion.12 = (f32[128]{0:T(128)S(1)}, f32[128,1024]{1,0:T(8,128)S(1)}) fusion(bf16[128,8192]{1,0:T(8,128)(2,1)} %multiply_convert_fusion, bf16[8192,1024]{1,0:T(8,128)(2,1)} %all-gather.2.cloned.1.call-done), kind=kOutput, calls=%fused_computation.30 | convolution fusion | flops 2147614720 | bytes 19399168 | tf_op jit(solution)/shard_map/dot_general | solution.py:17
  179.1 0.0 copy-start.4
  179.1 0.0 copy-start.3
  179.2 16.6 %gather_fusion = f32[2048]{0:T(1024)S(1)} fusion(f32[128,1024]{1,0:T(8,128)S(1)} %get-tuple-element.16, s32[2048]{0:T(1024)S(1)} %reshape.39), kind=kCustom, calls=%fused_computation | custom fusion | bytes 32768 | tf_op jit(solution)/shard_map/jit(take_along_axis)/gather | solution.py:27
  195.8 0.1 reshape.42
  195.9 0.0 copy-done.4
  195.9 0.2 select_reduce_fusion
  196.1 2.4 fusion.1
  198.5 124.6 %all-reduce.1 = (f32[128]{0:T(128)S(1)}, f32[128]{0:T(128)S(1)}) all-reduce(f32[128]{0:T(128)S(1)} %get-tuple-element.15, f32[128]{0:T(128)S(1)} %get-tuple-element.9), channel_id=1, replica_groups=mesh['prompt'=4,'vocab'=64] {'vocab'}, use_global_device_ids=true, to_apply=%region_7.8 | all-reduce | flops 256 | bytes 2048 | tf_op jit(solution)/shard_map/pmax | solution.py:30
  323.1 0.2 exponential_reduce_fusion.1
  323.3 0.2 exponential_reduce_fusion
  323.5 128.4 %all-reduce = (f32[128]{0:T(128)S(1)}, f32[128]{0:T(128)S(1)}) all-reduce(f32[128]{0:T(128)S(1)} %exponential_reduce_fusion, f32[128]{0:T(128)S(1)} %exponential_reduce_fusion.1), channel_id=1, replica_groups=mesh['prompt'=4,'vocab'=64] {'vocab'}, use_global_device_ids=true, to_apply=%region_9.10 | all-reduce | flops 256 | bytes 2048 | tf_op jit(solution)/shard_map/psum | solution.py:33
  452.0 0.5 fusion.10
  452.5 0.0 copy-done.3
  452.5 13.4 %fusion.2 = f32[128,8192]{1,0:T(8,128)} fusion(bf16[8192,1024]{1,0:T(8,128)(2,1)} %all-gather.2.cloned.1.call-done, f32[128,1024]{1,0:T(8,128)S(1)} %get-tuple-element.16, pred[128,1024]{1,0:T(8,128)(4,1)S(1)} %fusion.1, f32[128]{0:T(128)S(1)} %get-tuple-element.8, f32[128]{0:T(128)S(1)} %get-tuple-element.7, f32[128]{0:T(128)S(1)} %copy-done.3), kind=kOutput, calls=%fused_computation.8 | convolution fusion | flops 2148270080 | bytes 21628416 | tf_op jit(solution)/shard_map/dot_general | solution.py:48
  466.0 0.0 reduce-scatter.2.cloned.1.call-update
  466.0 2.3 convert_element_type.12
  468.3 0.1 dynamic_slice.9
  468.4 132.1 %reduce-scatter.2.cloned.1.call-done = f32[128,128]{1,0:T(8,128)} async-done(((f32[128,8192]{1,0:T(8,128)}), f32[128,128]{1,0:T(8,128)}) %reduce-scatter.2.cloned.1.call-update) | async-done | bytes 65552 | tf_op jit(solution)/shard_map/reduce_scatter | solution.py:54
  600.5 0.9 multiply_reduce_fusion.1
  601.5 129.2 %psum.23 = f32[128]{0:T(128)S(1)} all-reduce(f32[128]{0:T(128)S(1)} %multiply_reduce_fusion.1), channel_id=1, replica_groups=mesh['prompt'=4,'vocab'=64] {'vocab'}, use_global_device_ids=true, to_apply=%region_12.13 | all-reduce | flops 128 | bytes 1024 | tf_op jit(solution)/shard_map/psum | solution.py:56
  730.7 1.6 multiply_subtract_fusion
  (2 shorter events, 0.0 us)
Async XLA Ops:
  7.2 0.8 copy-start.2
  7.2 1.6 copy-start
  7.2 2.1 copy-start.1
  7.2 163.1 %all-gather.2.cloned.1.call-start = ((), (), s32[]{:S(2)}) async-start(), calls=%async_computation.1 | async-start | bytes 20971520 | tf_op jit(solution)/shard_map/all_gather | solution.py:19
  7.9 592.6 %reduce-scatter.2.cloned.1.call-start = ((), (), s32[]{:S(2)}) async-start(), calls=%async_computation.2 | async-start | bytes 4259840 | tf_op jit(solution)/shard_map/reduce_scatter | solution.py:54
  179.1 16.8 %copy-start.4 = (s32[128]{0:T(128)S(1)}, s32[128]{0:T(128)}, u32[]{:S(2)}) copy-start(s32[128]{0:T(128)} %param.10) | copy-start | bytes 1540
  179.1 273.4 %copy-start.3 = (f32[128]{0:T(128)S(1)}, f32[128]{0:T(128)}, u32[]{:S(2)}) copy-start(f32[128]{0:T(128)} %param.11) | copy-start | bytes 1540
Sparse Core Ops, SparseCore 0:
  9.8 160.4 all-gather.1
  466.1 134.3 reduce-scatter.1
where the time goes:
time: 739 us
  blocking collectives  382 us (52%)
  waiting for transfers between devices  292 us (40%)
  matrix products  22.3 us (3%)
  local copies, waits for them, and re-layouts  17.6 us (2%)
  between operations  14.2 us (2%)
  other arithmetic  10.9 us (1%)
    all_gather x1, waiting for transfers between devices, shards(): lax.all_gather(head, 'prompt', axis=0, tiled=True)  159 us
    reduce_scatter x1, waiting for transfers between devices, shards(): lax.psum_scatter(grad_full, 'vocab', scatter_dimension=1, tiled=True)  132 us
    psum x1, blocking collectives, shards(): row_term = lax.psum(jnp.sum(grad_cols * normed_cols, axis=1), 'vocab')  129 us
    psum x1, blocking collectives, shards(): sum_all, sum_ref = lax.psum((sum_all, sum_ref), 'vocab')  128 us
    pmax x1, blocking collectives, shards(): peak_all, peak_ref = lax.pmax((peak_all, peak_ref), 'vocab')  125 us
    gather x3, local copies, waits for them, and re-layouts, shards(): picked = jnp.take_along_axis(logits, safe_ids, axis=1)  16.8 us
  transfers between devices with their start and end apart: 2, of which 2 were waited for; matrix products, arithmetic and copies ran while one was open for 1% of the time, Pallas kernels for 0%

commit v1 on v0

--- a/solution.py
+++ b/solution.py
@@ -16,7 +16,9 @@
     normed = (hidden_f * inverse_rms * gain).astype(jnp.bfloat16)
     logits = jnp.dot(
         normed,
-        lax.all_gather(head, "prompt", axis=0, tiled=True),
+        jnp.concatenate(
+            lax.all_to_all(jnp.stack([head] * lax.axis_size("prompt")), "prompt", 0, 0), axis=0
+        ),
         preferred_element_type=jnp.float32,
     )
     vocab_start = lax.axis_index("vocab") * vocab_local

time: 739 us -> 910 us (1.23)
  waiting for transfers between devices: 292 us -> 444 us
    all_to_all x0 -> x1, waiting for transfers between devices: none -> 314 us  [shards(): lax.all_to_all(jnp.stack([head] * lax.axis_size('prompt')), 'prompt', 0, 0)]
    all_gather x1, waiting for transfers between devices: 159 us -> 0.02 us  [shards(): lax.all_gather(head, 'prompt', axis=0, tiled=True)]
  transfers between devices with their start and end apart: 2 -> 3, of which waited for: 2 -> 2; matrix products, arithmetic and copies ran while one was open for 1% -> 5% of each run, Pallas kernels for 0% -> 0%
where the time goes in v1:
time: 910 us
  waiting for transfers between devices  444 us (49%)
  blocking collectives  387 us (43%)
  local copies, waits for them, and re-layouts  24.5 us (3%)
  matrix products  22.3 us (2%)
  between operations  14.2 us (2%)
  other arithmetic  10.9 us (1%)
    all_to_all x1, waiting for transfers between devices, shards(): lax.all_to_all(jnp.stack([head] * lax.axis_size('prompt')), 'prompt', 0, 0)  314 us
    pmax x1, blocking collectives, shards(): peak_all, peak_ref = lax.pmax((peak_all, peak_ref), 'vocab')  130 us
    psum x1, blocking collectives, shards(): row_term = lax.psum(jnp.sum(grad_cols * normed_cols, axis=1), 'vocab')  129 us
    reduce_scatter x1, waiting for transfers between devices, shards(): lax.psum_scatter(grad_full, 'vocab', scatter_dimension=1, tiled=True)  129 us
    psum x1, blocking collectives, shards(): sum_all, sum_ref = lax.psum((sum_all, sum_ref), 'vocab')  128 us
  transfers between devices with their start and end apart: 3, of which 2 were waited for; matrix products, arithmetic and copies ran while one was open for 5% of the time, Pallas kernels for 0%

profile of v1, /device:TPU:1, one launch (start us, length us, event | category | flops | bytes accessed | tf_op | source)
XLA Modules:
  0.0 910.0 jit_solution(3506879918497108284)
XLA Ops:
  7.2 0.0 all-gather.2.cloned.1.call-start
  7.2 0.7 all-gather.2.cloned.1.call-update
  7.9 7.5 stack.2
  15.4 0.0 copy-start.2
  15.4 0.0 copy-start
  15.4 0.0 copy-start.1
  15.4 7.1 all-to-all-start
  22.5 0.0 reduce-scatter.2.cloned.1.call-start
  22.5 0.0 copy-done.2
  22.5 0.1 copy.11
  22.7 0.1 reshape.45
  22.8 0.0 copy-done
  22.8 0.5 multiply_reduce_fusion
  23.3 0.0 copy-done.1
  23.3 1.9 multiply_convert_fusion
  25.2 313.9 %all-to-all-done = bf16[4,2048,1024]{2,1,0:T(8,128)(2,1)} async-done(((bf16[4,2048,1024]{2,1,0:T(8,128)(2,1)}), bf16[4,2048,1024]{2,1,0:T(8,128)(2,1)}, u32[]{:S(2)}, u32[]{:S(2)}) %all-to-all-start) | async-done | bytes 16777248 | tf_op jit(solution)/shard_map/all_to_all | solution.py:20
  339.1 8.8 fusion.12
  347.9 0.0 copy-start.4
  347.9 0.0 copy-start.3
  348.0 16.6 %gather_fusion = f32[2048]{0:T(1024)S(1)} fusion(f32[128,1024]{1,0:T(8,128)S(1)} %get-tuple-element.16, s32[2048]{0:T(1024)S(1)} %reshape.45), kind=kCustom, calls=%fused_computation | custom fusion | bytes 32768 | tf_op jit(solution)/shard_map/jit(take_along_axis)/gather | solution.py:29
  364.6 0.1 reshape.48
  364.7 0.0 copy-done.4
  364.7 0.2 select_reduce_fusion
  364.9 130.4 %all-reduce.1 = (f32[128]{0:T(128)S(1)}, f32[128]{0:T(128)S(1)}) all-reduce(f32[128]{0:T(128)S(1)} %get-tuple-element.15, f32[128]{0:T(128)S(1)} %get-tuple-element.9), channel_id=1, replica_groups=mesh['prompt'=4,'vocab'=64] {'vocab'}, use_global_device_ids=true, to_apply=%region_7.8 | all-reduce | flops 256 | bytes 2048 | tf_op jit(solution)/shard_map/pmax | solution.py:32
  495.3 0.2 exponential_reduce_fusion.1
  495.5 0.2 exponential_reduce_fusion
  495.7 127.5 %all-reduce = (f32[128]{0:T(128)S(1)}, f32[128]{0:T(128)S(1)}) all-reduce(f32[128]{0:T(128)S(1)} %exponential_reduce_fusion, f32[128]{0:T(128)S(1)} %exponential_reduce_fusion.1), channel_id=1, replica_groups=mesh['prompt'=4,'vocab'=64] {'vocab'}, use_global_device_ids=true, to_apply=%region_9.10 | all-reduce | flops 256 | bytes 2048 | tf_op jit(solution)/shard_map/psum | solution.py:35
  623.3 0.5 fusion.10
  623.8 2.4 fusion.1
  626.2 0.0 all-gather.2.cloned.1.call-done
  626.2 0.0 copy-done.3
  626.2 13.5 %fusion.2 = f32[128,8192]{1,0:T(8,128)} fusion(bf16[8192,1024]{1,0:T(8,128)(2,1)} %all-gather.2.cloned.1.call-done, f32[128,1024]{1,0:T(8,128)S(1)} %get-tuple-element.16, pred[128,1024]{1,0:T(8,128)(4,1)S(1)} %fusion.1, f32[128]{0:T(128)S(1)} %get-tuple-element.8, f32[128]{0:T(128)S(1)} %get-tuple-element.7, f32[128]{0:T(128)S(1)} %copy-done.3), kind=kOutput, calls=%fused_computation.8 | convolution fusion | flops 2148270080 | bytes 21628416 | tf_op jit(solution)/shard_map/dot_general | solution.py:50
  639.7 0.0 reduce-scatter.2.cloned.1.call-update
  639.7 2.4 convert_element_type.12
  642.1 0.1 dynamic_slice.9
  642.1 129.2 %reduce-scatter.2.cloned.1.call-done = f32[128,128]{1,0:T(8,128)} async-done(((f32[128,8192]{1,0:T(8,128)}), f32[128,128]{1,0:T(8,128)}) %reduce-scatter.2.cloned.1.call-update) | async-done | bytes 65552 | tf_op jit(solution)/shard_map/reduce_scatter | solution.py:56
  771.4 0.9 multiply_reduce_fusion.1
  772.3 129.2 %psum.23 = f32[128]{0:T(128)S(1)} all-reduce(f32[128]{0:T(128)S(1)} %multiply_reduce_fusion.1), channel_id=1, replica_groups=mesh['prompt'=4,'vocab'=64] {'vocab'}, use_global_device_ids=true, to_apply=%region_12.13 | all-reduce | flops 128 | bytes 1024 | tf_op jit(solution)/shard_map/psum | solution.py:58
  901.6 1.6 multiply_subtract_fusion
  (2 shorter events, 0.0 us)
Async XLA Ops:
  7.2 619.1 %all-gather.2.cloned.1.call-start = ((), (), s32[]{:S(2)}) async-start(), calls=%async_computation.2 | async-start | bytes 20971520 | tf_op jit(solution)/shard_map/all_gather | solution.py:52
  15.4 7.2 copy-start.2
  15.4 7.4 copy-start
  15.4 7.9 copy-start.1
  15.4 323.7 %all-to-all-start = ((bf16[4,2048,1024]{2,1,0:T(8,128)(2,1)}), bf16[4,2048,1024]{2,1,0:T(8,128)(2,1)}, u32[]{:S(2)}, u32[]{:S(2)}) async-start(bf16[4,2048,1024]{2,1,0:T(8,128)(2,1)} %stack.2), calls=%async_computation | async-start | bytes 33554432 | tf_op jit(solution)/shard_map/all_to_all | solution.py:20
  22.5 748.9 %reduce-scatter.2.cloned.1.call-start = ((), (), s32[]{:S(2)}) async-start(), calls=%async_computation.3 | async-start | bytes 4259840 | tf_op jit(solution)/shard_map/reduce_scatter | solution.py:56
  347.9 16.8 %copy-start.4 = (s32[128]{0:T(128)S(1)}, s32[128]{0:T(128)}, u32[]{:S(2)}) copy-start(s32[128]{0:T(128)} %param.10) | copy-start | bytes 1540
  347.9 278.3 %copy-start.3 = (f32[128]{0:T(128)S(1)}, f32[128]{0:T(128)}, u32[]{:S(2)}) copy-start(f32[128]{0:T(128)} %param.11) | copy-start | bytes 1540
Sparse Core Ops, SparseCore 0:
  9.8 295.6 all-gather.1
  639.8 131.4 reduce-scatter.1

commit v2 on v0

--- a/solution.py
+++ b/solution.py
@@ -53,7 +53,7 @@
     )
     grad_cols = lax.psum_scatter(grad_full, "vocab", scatter_dimension=1, tiled=True)
     normed_cols = lax.dynamic_slice_in_dim(normed, col_start, slice_width, 1).astype(jnp.float32)
-    row_term = lax.psum(jnp.sum(grad_cols * normed_cols, axis=1), "vocab")
+    row_term = jnp.sum(lax.all_gather(jnp.sum(grad_cols * normed_cols, axis=1), "vocab"), axis=0)
     hidden_cols = lax.dynamic_slice_in_dim(hidden_f, col_start, slice_width, 1)
     gain_cols = lax.dynamic_slice_in_dim(gain, col_start, slice_width, 0)
     grad_hidden = (

time: 739 us -> 654 us (0.88)
  blocking collectives: 382 us -> 297 us
    psum x1 -> x0, blocking collectives: 129 us -> none  [shards(): row_term = lax.psum(jnp.sum(grad_cols * normed_cols, axis=1), 'vocab')]
    all_gather x0 -> x1, blocking collectives: none -> 43.7 us  [shards(): lax.all_gather(jnp.sum(grad_cols * normed_cols, axis=1), 'vocab')]
where the time goes in v2:
time: 654 us
  blocking collectives  297 us (45%)
  waiting for transfers between devices  292 us (45%)
  matrix products  22.3 us (3%)
  local copies, waits for them, and re-layouts  17.6 us (3%)
  between operations  14.2 us (2%)
  other arithmetic  11 us (2%)
    all_gather x1, waiting for transfers between devices, shards(): lax.all_gather(head, 'prompt', axis=0, tiled=True)  159 us
    reduce_scatter x1, waiting for transfers between devices, shards(): lax.psum_scatter(grad_full, 'vocab', scatter_dimension=1, tiled=True)  132 us
    psum x1, blocking collectives, shards(): sum_all, sum_ref = lax.psum((sum_all, sum_ref), 'vocab')  128 us
    pmax x1, blocking collectives, shards(): peak_all, peak_ref = lax.pmax((peak_all, peak_ref), 'vocab')  125 us
    all_gather x1, blocking collectives, shards(): lax.all_gather(jnp.sum(grad_cols * normed_cols, axis=1), 'vocab')  43.7 us
    gather x3, local copies, waits for them, and re-layouts, shards(): picked = jnp.take_along_axis(logits, safe_ids, axis=1)  16.8 us
    dot_general x1, matrix products, shards(): lax.dot_general(grad_b, lax.all_gather(head, 'prompt', axis=0, tiled=True...  13.4 us
  transfers between devices with their start and end apart: 2, of which 2 were waited for; matrix products, arithmetic and copies ran while one was open for 1% of the time, Pallas kernels for 0%

profile of v2, /device:TPU:1, one launch (start us, length us, event | category | flops | bytes accessed | tf_op | source)
XLA Modules:
  0.0 653.8 jit_solution(11738363051979935627)
XLA Ops:
  7.2 0.0 copy-start.2
  7.2 0.0 copy-start
  7.2 0.0 copy-start.1
  7.2 0.0 all-gather.4.cloned.1.call-start
  7.2 0.7 all-gather.4.cloned.1.call-update
  7.9 0.0 reduce-scatter.2.cloned.1.call-start
  8.0 0.0 copy-done.2
  8.0 0.1 copy.12
  8.1 0.1 reshape.39
  8.2 0.6 copy-done
  8.8 0.5 multiply_reduce_fusion
  9.3 0.0 copy-done.1
  9.3 1.9 multiply_convert_fusion
  11.2 159.1 %all-gather.4.cloned.1.call-done = bf16[8192,1024]{1,0:T(8,128)(2,1)} async-done(((bf16[2048,1024]{1,0:T(8,128)(2,1)}), bf16[8192,1024]{1,0:T(8,128)(2,1)}) %all-gather.4.cloned.1.call-update) | async-done | bytes 16777232 | tf_op jit(solution)/shard_map/all_gather | solution.py:19
  170.3 8.8 %fusion.12 = (f32[128]{0:T(128)S(1)}, f32[128,1024]{1,0:T(8,128)S(1)}) fusion(bf16[128,8192]{1,0:T(8,128)(2,1)} %multiply_convert_fusion, bf16[8192,1024]{1,0:T(8,128)(2,1)} %all-gather.4.cloned.1.call-done), kind=kOutput, calls=%fused_computation.30 | convolution fusion | flops 2147614720 | bytes 19399168 | tf_op jit(solution)/shard_map/dot_general | solution.py:17
  179.1 0.0 copy-start.4
  179.1 0.0 copy-start.3
  179.2 16.6 %gather_fusion = f32[2048]{0:T(1024)S(1)} fusion(f32[128,1024]{1,0:T(8,128)S(1)} %get-tuple-element.16, s32[2048]{0:T(1024)S(1)} %reshape.39), kind=kCustom, calls=%fused_computation | custom fusion | bytes 32768 | tf_op jit(solution)/shard_map/jit(take_along_axis)/gather | solution.py:27
  195.8 0.1 reshape.42
  195.9 0.0 copy-done.4
  195.9 0.2 select_reduce_fusion
  196.1 2.4 fusion.1
  198.5 124.6 %all-reduce.1 = (f32[128]{0:T(128)S(1)}, f32[128]{0:T(128)S(1)}) all-reduce(f32[128]{0:T(128)S(1)} %get-tuple-element.15, f32[128]{0:T(128)S(1)} %get-tuple-element.9), channel_id=1, replica_groups=mesh['prompt'=4,'vocab'=64] {'vocab'}, use_global_device_ids=true, to_apply=%region_7.8 | all-reduce | flops 256 | bytes 2048 | tf_op jit(solution)/shard_map/pmax | solution.py:30
  323.1 0.2 exponential_reduce_fusion.1
  323.3 0.2 exponential_reduce_fusion
  323.5 128.4 %all-reduce = (f32[128]{0:T(128)S(1)}, f32[128]{0:T(128)S(1)}) all-reduce(f32[128]{0:T(128)S(1)} %exponential_reduce_fusion, f32[128]{0:T(128)S(1)} %exponential_reduce_fusion.1), channel_id=1, replica_groups=mesh['prompt'=4,'vocab'=64] {'vocab'}, use_global_device_ids=true, to_apply=%region_9.10 | all-reduce | flops 256 | bytes 2048 | tf_op jit(solution)/shard_map/psum | solution.py:33
  452.0 0.5 fusion.10
  452.5 0.0 copy-done.3
  452.5 13.4 %fusion.2 = f32[128,8192]{1,0:T(8,128)} fusion(bf16[8192,1024]{1,0:T(8,128)(2,1)} %all-gather.4.cloned.1.call-done, f32[128,1024]{1,0:T(8,128)S(1)} %get-tuple-element.16, pred[128,1024]{1,0:T(8,128)(4,1)S(1)} %fusion.1, f32[128]{0:T(128)S(1)} %get-tuple-element.8, f32[128]{0:T(128)S(1)} %get-tuple-element.7, f32[128]{0:T(128)S(1)} %copy-done.3), kind=kOutput, calls=%fused_computation.8 | convolution fusion | flops 2148270080 | bytes 21628416 | tf_op jit(solution)/shard_map/dot_general | solution.py:48
  466.0 0.0 reduce-scatter.2.cloned.1.call-update
  466.0 2.4 convert_element_type.12
  468.3 0.1 dynamic_slice.9
  468.4 132.2 %reduce-scatter.2.cloned.1.call-done = f32[128,128]{1,0:T(8,128)} async-done(((f32[128,8192]{1,0:T(8,128)}), f32[128,128]{1,0:T(8,128)}) %reduce-scatter.2.cloned.1.call-update) | async-done | bytes 65552 | tf_op jit(solution)/shard_map/reduce_scatter | solution.py:54
  600.6 0.9 multiply_reduce_fusion.1
  601.5 43.7 %all-gather.1 = f32[64,1,128]{2,1,0:T(1,128)S(1)} all-gather(f32[1,1,128]{2,1,0:T(1,128)S(1)} %bitcast.8), channel_id=2, replica_groups=mesh['prompt'=4,'vocab'=64] {'vocab'}, dimensions={0}, use_global_device_ids=true | all-gather | bytes 33280 | tf_op jit(solution)/shard_map/all_gather | solution.py:56
  645.2 0.1 reduce_sum.49
  645.3 1.6 multiply_subtract_fusion
  (2 shorter events, 0.0 us)
Async XLA Ops:
  7.2 0.8 copy-start.2
  7.2 1.6 copy-start
  7.2 2.1 copy-start.1
  7.2 163.1 %all-gather.4.cloned.1.call-start = ((), (), s32[]{:S(2)}) async-start(), calls=%async_computation.1 | async-start | bytes 20971520 | tf_op jit(solution)/shard_map/all_gather | solution.py:19
  7.9 592.6 %reduce-scatter.2.cloned.1.call-start = ((), (), s32[]{:S(2)}) async-start(), calls=%async_computation.2 | async-start | bytes 4259840 | tf_op jit(solution)/shard_map/reduce_scatter | solution.py:54
  179.1 16.8 %copy-start.4 = (s32[128]{0:T(128)S(1)}, s32[128]{0:T(128)}, u32[]{:S(2)}) copy-start(s32[128]{0:T(128)} %param.10) | copy-start | bytes 1540
  179.1 273.4 %copy-start.3 = (f32[128]{0:T(128)S(1)}, f32[128]{0:T(128)}, u32[]{:S(2)}) copy-start(f32[128]{0:T(128)} %param.11) | copy-start | bytes 1540
Sparse Core Ops, SparseCore 0:
  9.8 160.4 all-gather.3
  466.1 134.4 reduce-scatter.1
